TPU v7x, 128 devices: a whole 4x4x4 slice. The times are simulated.
128 devices in a mesh: inp: 8 (over z, x_hi), tm: 8 (over x_lo, y), bl: 2 (over core).
Axes of the slice: x: 4 (x_hi: 2, x_lo: 2; x = x_hi * 2 + x_lo), y: 4, z: 4, core: 2. Of those that a mesh axis runs over, the one named last changes fastest.
Arguments:
- voltages: int32 [1024, 524288], P(('inp', 'bl'), 'tm'), may hold values from -16 to 14, as said below
- taps: float32 [4, 16384], replicated, may hold values from -3 to 3
- flags: int32 [1024], P(('inp', 'bl')), may hold values 0 or 1
Outputs:
- visibilities: float32 [2, 128, 8, 128, 1024], P(None, ('inp', 'tm'), None, 'bl')
Inputs may be any that keep to these rules, and one draw needn't show every extreme that they name: `voltages`: int8-valued digitized samples, each input's stream in time order.
All inputs are finite; a program needn't handle non-finite values. No bound on the sum of `flags` on one device may be relied on, other than what follows from the above.
Results may differ from a plain program's by a relative error of at most 0.00065.
Values may be sent and summed in bfloat16 or wider, within the bound.
A program may use at most 192 MiB of HBM per device.

v0:
```python
import math
import jax
import jax.numpy as jnp
from jax import lax
from jax.sharding import PartitionSpec as P

CH_AVG = 64
FIRST = 128


def passed_along(value, axis, steps):
    count = lax.axis_size(axis)
    initial, last = (max(0, -steps), min(count, count - steps))
    return lax.ppermute(value, axis, [(source, source + steps) for source in range(initial, last)])


def cos_sin(height, breadth, period):
    grid = lax.broadcasted_iota(jnp.int32, (height, breadth), 0) * lax.broadcasted_iota(
        jnp.int32, (height, breadth), 1
    )
    angle = (grid % period).astype(jnp.float32) * (2.0 * math.pi / period)
    return (jnp.cos(angle), jnp.sin(angle))


def transform(blocks, length, precision):
    first_len = FIRST
    second_len = length // first_len
    highs = length // 2 // first_len
    cos_one, sin_one = cos_sin(first_len, first_len, first_len)
    table_one = jnp.stack([cos_one, -sin_one])
    section_one = jnp.einsum("xca,mab->xmcb", table_one, blocks, precision=precision)
    cos_twist, sin_twist = cos_sin(first_len, second_len, length)
    real_one = section_one[0]
    imag_one = section_one[1]
    twisted = jnp.stack(
        [real_one * cos_twist + imag_one * sin_twist, imag_one * cos_twist - real_one * sin_twist]
    )
    cos_two, sin_two = cos_sin(highs, second_len, second_len)
    table_two = jnp.stack(
        [jnp.stack([cos_two, sin_two], axis=1), jnp.stack([-sin_two, cos_two], axis=1)]
    )
    return jnp.einsum("yqxb,xmcb->yqmc", table_two, twisted, precision=precision)


def shards(voltages, taps, flags):
    inputs = voltages.shape[0]
    tap_count = taps.shape[0]
    length = taps.shape[1]
    second_len = length // FIRST
    spectra_dev = voltages.shape[1] // length
    reach = tap_count - 1
    local = spectra_dev - reach
    precision = lax.Precision.HIGH
    blocked = voltages.reshape(inputs, spectra_dev, FIRST, second_len)
    leading = blocked[:, :reach].astype(jnp.bfloat16)
    following = passed_along(leading, "tm", -1)
    samples = blocked.astype(jnp.float32)
    tap_blocks = taps.reshape(tap_count, FIRST, second_len)

    def filtered(pieces, count):
        rows = []
        for spectrum in range(count):
            total = jnp.zeros((inputs, FIRST, second_len), jnp.float32)
            for offset in range(tap_count):
                total = total + tap_blocks[offset][None] * pieces[spectrum + offset]
            rows.append(total)
        return jnp.concatenate(rows, axis=0)

    own_pieces = [samples[:, j] for j in range(spectra_dev)]
    next_pieces = [following[:, j].astype(jnp.float32) for j in range(reach)]
    first_part = transform(filtered(own_pieces, local), length, precision)
    second_part = transform(filtered(own_pieces[local:] + next_pieces, reach), length, precision)
    both_parts = jnp.concatenate([first_part, second_part], axis=2)
    scale = jnp.tile(flags.astype(jnp.float32) / (8.0 * math.sqrt(length)), spectra_dev)
    spectra = (both_parts * scale[None, None, :, None]).astype(jnp.bfloat16)
    turned = lax.all_to_all(spectra, ("inp", "tm"), split_axis=1, concat_axis=1, tiled=True)
    groups_inp = lax.axis_size("inp")
    groups_tm = lax.axis_size("tm")
    out_groups = FIRST // CH_AVG
    rows = turned.reshape(2, groups_inp, groups_tm, spectra_dev, inputs, FIRST)
    own = jnp.transpose(rows, (1, 4, 0, 2, 3, 5)).reshape(groups_inp, inputs, -1)
    half = own.shape[-1] // 2
    swapped = jnp.concatenate([own[..., half:], -own[..., :half]], axis=-1)
    lane_group = lax.broadcasted_iota(jnp.int32, (out_groups, own.shape[-1]), 1) % FIRST // CH_AVG
    mask = lane_group == lax.broadcasted_iota(jnp.int32, (out_groups, own.shape[-1]), 0)
    mask = mask.astype(own.dtype)
    lhs = jnp.stack([own, swapped])[:, None] * mask[None, :, None, None, :]
    columns = lax.all_gather(own, "bl", axis=1, tiled=True).reshape(-1, own.shape[-1])
    count = float(groups_tm * spectra_dev * CH_AVG)
    products = jnp.einsum("xgpik,qk->xgpiq", lhs, columns, preferred_element_type=jnp.float32)
    return products * (1.0 / count)


def solution(mesh):
    in_specs = (P(("inp", "bl"), "tm"), P(), P(("inp", "bl")))
    out_specs = P(None, ("inp", "tm"), None, "bl", None)
    return jax.shard_map(shards, mesh=mesh, in_specs=in_specs, out_specs=out_specs, check_vma=False)
```

profile of v0, /device:TPU:2, one launch (start us, length us, event | category | flops | bytes accessed | tf_op | source)
XLA Modules:
  0.0 504.2 jit_solution(362682598263856912)
XLA Ops:
  6.5 21.8 %convert_bitcast_fusion.1 = (bf16[8,8,512,128]{3,1,2,0:T(8,128)(2,1)}, f32[8,8,512,128]{3,1,2,0:T(8,128)}) fusion(s32[64,65536]{1,0:T(8,128)} %param.3), kind=kLoop, calls=%fused_computation.27 | loop fusion | flops 8388608 | bytes 41943040
  28.3 9.0 %copy.51 = bf16[8,8,512,128]{3,2,1,0:T(8,128)(2,1)} copy(bf16[8,8,512,128]{3,1,2,0:T(8,128)(2,1)} %get-tuple-element.11) | data formatting | bytes 16777216
  37.3 8.1 %slice.95 = bf16[64,3,128,128]{3,2,1,0:T(8,128)(2,1)} slice(bf16[64,4,128,128]{3,2,1,0:T(8,128)(2,1)} %bitcast.155), slice={[0:64], [0:3], [0:128], [0:128]} | slice | bytes 12582912 | tf_op jit(solution)/shard_map/slice | solution.py:55
  45.4 8.6 %copy.49 = bf16[64,3,128,128]{2,3,0,1:T(8,128)(2,1)} copy(bf16[64,3,128,128]{3,2,1,0:T(8,128)(2,1)} %slice.95) | data formatting | bytes 12582912
  54.0 5.2 %collective-permute-start = (bf16[64,3,128,128]{2,3,0,1:T(8,128)(2,1)}, bf16[64,3,128,128]{2,3,0,1:T(8,128)(2,1)}, u32[]{:S(2)}, u32[]{:S(2)}) collective-permute-start(bf16[64,3,128,128]{2,3,0,1:T(8,128)(2,1)} %copy.49), channel_id=1, source_target_pairs={{2,0},{4,2},{6,4},{8,6},{10,8},{12,10},{14,12},{3,1},{5,3},{7,5},{... | collective-permute-start | bytes 18874376 | tf_op jit(solution)/shard_map/ppermute | solution.py:14
  59.2 9.4 %copy.50 = f32[8,8,512,128]{3,2,1,0:T(8,128)S(1)} copy(f32[8,8,512,128]{3,1,2,0:T(8,128)} %get-tuple-element.12) | data formatting | bytes 33554432
  68.6 6.0 %fusion.77 = (f32[64,1,128,128]{3,2,1,0:T(8,128)}, f32[64,1,128,128]{3,2,1,0:T(8,128)}, f32[64,1,128,128]{3,2,1,0:T(8,128)}, f32[64,1,128,128]{3,2,1,0:T(8,128)}) fusion(f32[64,4,128,128]{3,2,1,0:T(8,128)S(1)} %bitcast.153), kind=kLoop, calls=%fused_computation.128 | loop fusion | bytes 33554432 | tf_op jit(solution)/shard_map/slice | solution.py:69
  74.6 5.6 %copy.46 = f32[64,1,128,128]{2,3,0,1:T(8,128)} copy(f32[64,1,128,128]{3,2,1,0:T(8,128)} %get-tuple-element.9) | data formatting | bytes 8388608
  80.3 5.7 %copy.47 = f32[64,1,128,128]{2,3,0,1:T(8,128)} copy(f32[64,1,128,128]{3,2,1,0:T(8,128)} %get-tuple-element.8) | data formatting | bytes 8388608
  85.9 5.6 %copy.48 = f32[64,1,128,128]{2,3,0,1:T(8,128)} copy(f32[64,1,128,128]{3,2,1,0:T(8,128)} %get-tuple-element.10) | data formatting | bytes 8388608
  91.5 5.6 %copy.45 = f32[64,1,128,128]{2,3,0,1:T(8,128)} copy(f32[64,1,128,128]{3,2,1,0:T(8,128)} %get-tuple-element.7) | data formatting | bytes 8388608
  98.2 0.3 sine_negate_fusion
  98.5 0.3 fusion.63
  98.8 8.0 %fusion.37 = f32[2,64,128,128]{2,3,0,1:T(8,128)S(1)} fusion(f32[64,1,128,128]{2,3,0,1:T(8,128)} %copy.48, f32[64,1,128,128]{2,3,0,1:T(8,128)} %copy.47, f32[64,1,128,128]{2,3,0,1:T(8,128)} %copy.46, f32[64,1,128,128]{2,3,0,1:T(8,128)} %copy.45, f32[128,128]{0,1:T(8,128)S(1)} %copy.28, f32[128,128]{0,1:T(8,128)S(1)} %copy.26, f32[128,128]{0,1:T(8,128)S(1)} %copy.24, ...), kind=kOutput, calls=%fused_computation.63 | convolution fusion | flops 1617985536 | bytes 25559040 | tf_op jit(solution)/shard_map/xca,mab->xmcb/dot_general | solution.py:31
  106.7 1.2 multiply_add_fusion.1
  108.0 4.4 fusion.40
  112.3 81.6 %collective-permute-done = bf16[64,3,128,128]{2,3,0,1:T(8,128)(2,1)} collective-permute-done((bf16[64,3,128,128]{2,3,0,1:T(8,128)(2,1)}, bf16[64,3,128,128]{2,3,0,1:T(8,128)(2,1)}, u32[]{:S(2)}, u32[]{:S(2)}) %collective-permute-start) | collective-permute-done | bytes 6291488 | tf_op jit(solution)/shard_map/ppermute | solution.py:14
  194.0 8.2 %fusion.21 = (f32[64,128,128]{1,2,0:T(8,128)}, f32[64,128,128]{1,2,0:T(8,128)}, f32[64,128,128]{1,2,0:T(8,128)}) fusion(f32[64,1,128,128]{2,3,0,1:T(8,128)S(1)} %copy-done.2, f32[64,1,128,128]{2,3,0,1:T(8,128)S(1)} %copy-done.1, f32[64,1,128,128]{2,3,0,1:T(8,128)S(1)} %copy-done, f32[128,128]{0,1:T(8,128)S(1)} %copy.28, f32[128,128]{0,1:T(8,128)S(1)} %copy.26, ...), kind=kLoop, calls=%fused_computation.37 | loop fusion | flops 25165824 | bytes 31719424 | tf_op jit(solution)/shard_map/add | solution.py:65
  202.2 18.0 %fusion.13 = f32[2,192,128,128]{2,3,0,1:T(8,128)} fusion(f32[64,128,128]{1,2,0:T(8,128)} %get-tuple-element.15, f32[64,128,128]{1,2,0:T(8,128)} %get-tuple-element.14, f32[64,128,128]{1,2,0:T(8,128)} %get-tuple-element.13, f32[1,128,128]{2,1,0:T(8,128)S(1)} %get-tuple-element.26, f32[1,128,128]{2,1,0:T(8,128)S(1)} %get-tuple-element.27), kind=kOutput, calls=%fused_computation.20 | convolution fusion | flops 4838162432 | bytes 37879808 | tf_op jit(solution)/shard_map/xca,mab->xmcb/dot_general | solution.py:31
  220.2 19.8 %multiply_add_fusion = (f32[1,192,128,128]{2,3,0,1:T(8,128)}, f32[1,192,128,128]{2,3,0,1:T(8,128)}) fusion(f32[2,192,128,128]{2,3,0,1:T(8,128)} %fusion.13, f32[128,128]{0,1:T(8,128)S(1)} %get-tuple-element.28, f32[128,128]{0,1:T(8,128)S(1)} %get-tuple-element.29), kind=kLoop, calls=%fused_computation.19 | loop fusion | flops 18874368 | bytes 50462720 | tf_op jit(solution)/shard_map/add | solution.py:36
  240.0 16.6 %fusion.17 = f32[2,64,192,128]{3,1,2,0:T(8,128)} fusion(f32[1,192,128,128]{2,3,0,1:T(8,128)} %get-tuple-element.6, f32[1,192,128,128]{2,3,0,1:T(8,128)} %get-tuple-element.5, f32[1,64,2,128]{3,1,2,0:T(8,128)S(1)} %get-tuple-element.25, f32[1,64,2,128]{3,1,2,0:T(8,128)S(1)} %get-tuple-element.24), kind=kOutput, calls=%fused_computation.33 | convolution fusion | flops 4838162432 | bytes 37879808 | tf_op jit(solution)/shard_map/yqxb,xmcb->yqmc/dot_general | solution.py:42
  256.6 9.0 %fusion.5 = bf16[2,64,256,128]{3,1,2,0:T(8,128)(2,1)} fusion(f32[2,64,192,128]{3,1,2,0:T(8,128)} %fusion.17, f32[2,64,64,128]{3,1,2,0:T(8,128)S(1)} %copy-done.3, f32[256]{0:T(256)S(1)} %mul.388), kind=kLoop, calls=%fused_computation.7 | loop fusion | flops 12582912 | bytes 25166848 | tf_op jit(solution)/shard_map/convert_element_type | solution.py:75
  265.6 12.0 %copy.33 = bf16[2,64,256,128]{3,2,0,1:T(8,128)(2,1)} copy(bf16[2,64,256,128]{3,1,2,0:T(8,128)(2,1)} %fusion.5) | data formatting | bytes 16777216 | tf_op jit(solution)/shard_map/convert_element_type | solution.py:75
  277.6 110.1 %all_to_all.5 = bf16[2,64,256,128]{3,2,0,1:T(8,128)(2,1)S(1)} all-to-all(bf16[2,64,256,128]{3,2,0,1:T(8,128)(2,1)} %copy.33), channel_id=1, replica_groups=mesh['inp'=8,'tm'=8,'bl'=2] {'inp','tm'}, dimensions={1} | all-to-all | bytes 16777216 | tf_op jit(solution)/shard_map/all_to_all | solution.py:76
  387.8 7.3 %copy.53 = bf16[2,8,8,4,64,128]{5,3,2,0,4,1:T(4,128)(2,1)} copy(bf16[2,8,8,4,64,128]{5,4,3,0,2,1:T(8,128)(2,1)S(1)} %bitcast.154) | data formatting | bytes 16777216 | tf_op jit(solution)/shard_map/reshape | solution.py:80
  395.1 14.4 %reshape.241 = bf16[8,64,8192]{2,1,0:T(8,128)(2,1)} reshape(bf16[8,64,2,8,4,128]{5,4,3,2,1,0:T(4,128)(2,1)} %bitcast.151) | data formatting | bytes 16777216 | tf_op jit(solution)/shard_map/reshape | solution.py:81
  409.5 0.2 compare_convert_fusion
  409.7 15.1 %stack_reshape.3 = bf16[1,8,64,8192]{3,2,1,0:T(8,128)(2,1)} reshape(bf16[8,64,2,8,4,128]{5,4,3,2,1,0:T(4,128)(2,1)} %bitcast.152) | data formatting | bytes 16777216 | tf_op jit(solution)/shard_map/stack;reshape | solution.py:87
  424.9 8.2 %fusion.78 = (bf16[8,64,4096]{2,1,0:T(8,128)(2,1)}, bf16[8,64,4096]{2,1,0:T(8,128)(2,1)}) fusion(bf16[8,64,8192]{2,1,0:T(8,128)(2,1)} %reshape.241), kind=kLoop, calls=%fused_computation.129 | loop fusion | flops 2097152 | bytes 16777216 | tf_op jit(solution)/shard_map/slice | solution.py:83
  433.1 7.9 %maximum_bitcast_fusion.8 = bf16[1,8,64,8192]{3,2,1,0:T(8,128)(2,1)} fusion(bf16[8,64,4096]{2,1,0:T(8,128)(2,1)} %get-tuple-element.19, bf16[8,64,4096]{2,1,0:T(8,128)(2,1)} %get-tuple-element.18), kind=kLoop, calls=%fused_computation.25 | loop fusion | flops 16777216 | bytes 16777216 | tf_op jit(solution)/shard_map/stack | solution.py:87
  440.9 13.8 %pad_maximum_fusion = bf16[2,8,64,8192]{3,2,1,0:T(8,128)(2,1)} fusion(bf16[1,8,64,8192]{3,2,1,0:T(8,128)(2,1)} %maximum_bitcast_fusion.8, bf16[1,8,64,8192]{3,2,1,0:T(8,128)(2,1)} %stack_reshape.3), kind=kLoop, calls=%fused_computation.8 | loop fusion | flops 8388608 | bytes 33554432 | tf_op jit(solution)/shard_map/stack | solution.py:87
  454.7 42.5 %broadcast_multiply_fusion = f32[2,2,8,64,1024]{4,3,2,1,0:T(8,128)} fusion(bf16[1024,8192,1,1,1]{1,0,4,3,2:T(8,128)(2,1)} %bitcast.160, bf16[2,8192]{1,0:T(2,128)(2,1)S(1)} %compare_convert_fusion, bf16[2,8,64,8192]{3,2,1,0:T(8,128)(2,1)} %pad_maximum_fusion), kind=kOutput, calls=%fused_computation.60 | convolution fusion | flops 34378612736 | bytes 41975808 | tf_op jit(solution)/shard_map/xgpik,qk->xgpiq/dot_general | solution.py:90
  (28 shorter events, 1.0 us)
Async XLA Ops:
  6.5 448.2 %all-gather.2.cloned.1.call-start = ((), (), s32[]{:S(2)}) async-start(), calls=%async_computation.1 | async-start | bytes 25165824 | tf_op jit(solution)/shard_map/all_gather | solution.py:88
  54.0 140.0 %collective-permute-start = (bf16[64,3,128,128]{2,3,0,1:T(8,128)(2,1)}, bf16[64,3,128,128]{2,3,0,1:T(8,128)(2,1)}, u32[]{:S(2)}, u32[]{:S(2)}) collective-permute-start(bf16[64,3,128,128]{2,3,0,1:T(8,128)(2,1)} %copy.49), channel_id=1, source_target_pairs={{2,0},{4,2},{6,4},{8,6},{10,8},{12,10},{14,12},{3,1},{5,3},{7,5},{... | collective-permute-start | bytes 18874376 | tf_op jit(solution)/shard_map/ppermute | solution.py:14
  91.5 5.6 %copy-start.4 = (f32[4,16384]{1,0:T(4,128)S(1)}, f32[4,16384]{1,0:T(4,128)}, u32[]{:S(2)}) copy-start(f32[4,16384]{1,0:T(4,128)} %param.4) | copy-start | bytes 786436
  91.5 6.2 %copy-start.5 = (s32[64]{0:T(128)S(1)}, s32[64]{0:T(128)}, u32[]{:S(2)}) copy-start(s32[64]{0:T(128)} %param.5) | copy-start | bytes 772
  107.9 86.1 %copy-start = (f32[64,1,128,128]{2,3,0,1:T(8,128)S(1)}, f32[64,1,128,128]{2,3,0,1:T(8,128)}, u32[]{:S(2)}) copy-start(f32[64,1,128,128]{2,3,0,1:T(8,128)} %copy.46) | copy-start | bytes 12582916
  107.9 86.1 %copy-start.1 = (f32[64,1,128,128]{2,3,0,1:T(8,128)S(1)}, f32[64,1,128,128]{2,3,0,1:T(8,128)}, u32[]{:S(2)}) copy-start(f32[64,1,128,128]{2,3,0,1:T(8,128)} %copy.47) | copy-start | bytes 12582916
  107.9 86.0 %copy-start.2 = (f32[64,1,128,128]{2,3,0,1:T(8,128)S(1)}, f32[64,1,128,128]{2,3,0,1:T(8,128)}, u32[]{:S(2)}) copy-start(f32[64,1,128,128]{2,3,0,1:T(8,128)} %copy.48) | copy-start | bytes 12582916
  240.0 16.6 %copy-start.3 = (f32[2,64,64,128]{3,1,2,0:T(8,128)S(1)}, f32[2,64,64,128]{3,1,2,0:T(8,128)}, u32[]{:S(2)}) copy-start(f32[2,64,64,128]{3,1,2,0:T(8,128)} %fusion.40) | copy-start | bytes 12582916
Sparse Core Ops, SparseCore 0:
  409.6 29.6 all-gather.1
where the time goes:
time: 509 us; the launch traced here: 504 us
  local copies, waits for them, and re-layouts  113 us (22%)
  blocking collectives  110 us (22%)
  other arithmetic  90.9 us (18%)
  matrix products  89.4 us (18%)
  waiting for transfers between devices  81.7 us (16%)
  between operations  13.8 us (3%)
  starting transfers between devices  5.18 us (1%)
    all_to_all x1, blocking collectives, shards(): lax.all_to_all(spectra, ('inp', 'tm'), split_axis=1, concat_axis=1, tiled...  110 us
    ppermute x1, waiting for transfers between devices, passed_along(): lax.ppermute(value, axis, [(source, source + steps) for source in range(i...  81.6 us
    unnamed x19, local copies, waits for them, and re-layouts  49.5 us
    dot_general x1, matrix products, shards(): jnp.einsum('xgpik,qk->xgpiq', lhs, columns, preferred_element_type=jnp.fl...  42.5 us
    dot_general x2, matrix products, transform(): jnp.einsum('xca,mab->xmcb', table_one, blocks, precision=precision)  26 us
    unnamed x1, other arithmetic  21.8 us
    another operation x2, other arithmetic, shards(): lhs = jnp.stack([own, swapped])[:, None] * mask[None, :, None, None, :]  21.6 us
    dot_general x2, matrix products, transform(): jnp.einsum('yqxb,xmcb->yqmc', table_two, twisted, precision=precision)  21 us
  transfers between devices with their start and end apart: 2, of which 1 were waited for; matrix products, arithmetic and copies ran while one was open for 19% of the time, Pallas kernels for 0%

commit v1 on v0

--- a/solution.py
+++ b/solution.py
@@ -73,7 +73,12 @@
     both_parts = jnp.concatenate([first_part, second_part], axis=2)
     scale = jnp.tile(flags.astype(jnp.float32) / (8.0 * math.sqrt(length)), spectra_dev)
     spectra = (both_parts * scale[None, None, :, None]).astype(jnp.bfloat16)
-    turned = lax.all_to_all(spectra, ("inp", "tm"), split_axis=1, concat_axis=1, tiled=True)
+    turned = jnp.concatenate(
+        lax.all_to_all(
+            jnp.stack(jnp.split(spectra, lax.axis_size(("inp", "tm")), axis=1)), ("inp", "tm"), 0, 0
+        ),
+        axis=1,
+    )
     groups_inp = lax.axis_size("inp")
     groups_tm = lax.axis_size("tm")
     out_groups = FIRST // CH_AVG

time: 509 us -> 537 us (1.055)
  local copies, waits for them, and re-layouts: 113 us -> 130 us
  other arithmetic: 90.9 us -> 104 us
    unnamed x19 -> x71, local copies, waits for them, and re-layouts: 49.5 us -> 20.3 us
    slice x1 -> x5, local copies, waits for them, and re-layouts: 6.02 us -> 28.7 us  [shards(): own_pieces = [samples[:, j] for j in range(spectra_dev)]]
    split x0 -> x4, local copies, waits for them, and re-layouts: none -> 18 us  [shards(): jnp.split(spectra, lax.axis_size(('inp', 'tm')), axis=1)]
    convert_element_type x0 -> x1, other arithmetic: none -> 7.99 us  [shards(): next_pieces = [following[:, j].astype(jnp.float32) for j in range(reach)]]
    reshape x1 -> x0, local copies, waits for them, and re-layouts: 7.28 us -> none  [shards(): rows = turned.reshape(2, groups_inp, groups_tm, spectra_dev, inputs, FIRST)]
    transpose x0 -> x1, local copies, waits for them, and re-layouts: none -> 7.28 us  [shards(): jnp.transpose(rows, (1, 4, 0, 2, 3, 5)).reshape(groups_inp, inputs, -1)]
    add x1, other arithmetic: 8.21 us -> 14.5 us  [filtered(): total = total + tap_blocks[offset][None] * pieces[spectrum + offset]]
    convert_element_type x1 -> x3, local copies, waits for them, and re-layouts: 12 us -> 16.9 us  [shards(): next_pieces = [following[:, j].astype(jnp.float32) for j in range(reach)]]
where the time goes in v1:
time: 537 us; the launch traced here: 533 us
  local copies, waits for them, and re-layouts  130 us (24%)
  blocking collectives  110 us (20%)
  other arithmetic  104 us (19%)
  matrix products  89 us (17%)
  waiting for transfers between devices  81 us (15%)
  between operations  14.2 us (3%)
    all_to_all x1, blocking collectives, shards(): lax.all_to_all(jnp.stack(jnp.split(spectra, lax.axis_size(('inp', 'tm')),...  110 us
    ppermute x1, waiting for transfers between devices, passed_along(): lax.ppermute(value, axis, [(source, source + steps) for source in range(i...  80.9 us
    dot_general x1, matrix products, shards(): jnp.einsum('xgpik,qk->xgpiq', lhs, columns, preferred_element_type=jnp.fl...  42.5 us
    slice x5, local copies, waits for them, and re-layouts, shards(): own_pieces = [samples[:, j] for j in range(spectra_dev)]  28.7 us
    dot_general x2, matrix products, transform(): jnp.einsum('xca,mab->xmcb', table_one, blocks, precision=precision)  25.4 us
    unnamed x1, other arithmetic  21.8 us
    another operation x2, other arithmetic, shards(): lhs = jnp.stack([own, swapped])[:, None] * mask[None, :, None, None, :]  21.6 us
    add x2, other arithmetic, transform(): real_one * cos_twist + imag_one * sin_twist  21.6 us
  transfers between devices with their start and end apart: 2, of which 1 were waited for; matrix products, arithmetic and copies ran while one was open for 19% of the time, Pallas kernels for 0%

profile of v1, /device:TPU:2, one launch (start us, length us, event | category | flops | bytes accessed | tf_op | source)
XLA Modules:
  0.0 532.6 jit_solution(14981294532154656845)
XLA Ops:
  6.5 21.8 %convert_bitcast_fusion = (f32[8,8,512,128]{3,1,2,0:T(8,128)}, bf16[8,8,512,128]{3,1,2,0:T(8,128)(2,1)}) fusion(s32[64,65536]{1,0:T(8,128)} %param.3), kind=kLoop, calls=%fused_computation.9 | loop fusion | flops 8388608 | bytes 41943040
  28.3 9.0 %copy.1948 = bf16[8,8,512,128]{3,2,1,0:T(8,128)(2,1)} copy(bf16[8,8,512,128]{3,1,2,0:T(8,128)(2,1)} %get-tuple-element.12) | data formatting | bytes 16777216
  37.3 8.2 %slice.95 = bf16[64,3,128,128]{3,2,1,0:T(8,128)(2,1)} slice(bf16[64,4,128,128]{3,2,1,0:T(8,128)(2,1)} %bitcast.288), slice={[0:64], [0:3], [0:128], [0:128]} | slice | bytes 12582912 | tf_op jit(solution)/shard_map/slice | solution.py:55
  45.5 5.2 collective-permute-start
  51.4 9.4 %copy.1947 = f32[8,8,512,128]{3,2,1,0:T(8,128)S(1)} copy(f32[8,8,512,128]{3,1,2,0:T(8,128)} %get-tuple-element.11) | data formatting | bytes 33554432
  60.8 6.2 %fusion.77 = (f32[64,1,128,128]{3,2,1,0:T(8,128)}, f32[64,1,128,128]{3,2,1,0:T(8,128)}, f32[64,1,128,128]{3,2,1,0:T(8,128)}, f32[64,1,128,128]{3,2,1,0:T(8,128)}) fusion(f32[64,4,128,128]{3,2,1,0:T(8,128)S(1)} %bitcast.286), kind=kLoop, calls=%fused_computation.191 | loop fusion | bytes 33554432 | tf_op jit(solution)/shard_map/slice | solution.py:69
  66.9 5.6 %copy.1859 = f32[64,1,128,128]{2,3,0,1:T(8,128)} copy(f32[64,1,128,128]{3,2,1,0:T(8,128)} %get-tuple-element.7) | data formatting | bytes 8388608 | tf_op jit(solution)/shard_map/slice | solution.py:69
  72.5 5.6 %copy.1865 = f32[64,1,128,128]{2,3,0,1:T(8,128)} copy(f32[64,1,128,128]{3,2,1,0:T(8,128)} %get-tuple-element.8) | data formatting | bytes 8388608 | tf_op jit(solution)/shard_map/slice | solution.py:69
  78.2 5.6 %copy.1863 = f32[64,1,128,128]{2,3,0,1:T(8,128)} copy(f32[64,1,128,128]{3,2,1,0:T(8,128)} %get-tuple-element.9) | data formatting | bytes 8388608 | tf_op jit(solution)/shard_map/slice | solution.py:69
  83.8 5.7 %copy.1861 = f32[64,1,128,128]{2,3,0,1:T(8,128)} copy(f32[64,1,128,128]{3,2,1,0:T(8,128)} %get-tuple-element.10) | data formatting | bytes 8388608 | tf_op jit(solution)/shard_map/slice | solution.py:69
  90.3 7.9 %fusion.37 = f32[2,64,128,128]{2,3,0,1:T(8,128)S(1)} fusion(f32[64,1,128,128]{2,3,0,1:T(8,128)} %copy.1865, f32[64,1,128,128]{2,3,0,1:T(8,128)} %copy.1863, f32[64,1,128,128]{2,3,0,1:T(8,128)} %copy.1861, f32[64,1,128,128]{2,3,0,1:T(8,128)} %copy.1859, f32[128,128]{0,1:T(8,128)S(1)} %copy.1864, f32[128,128]{0,1:T(8,128)S(1)} %copy.1862, ...), kind=kOutput, calls=%fused_computation.62 | convolution fusion | flops 1617985536 | bytes 25559040 | tf_op jit(solution)/shard_map/xca,mab->xmcb/dot_general | solution.py:31
  104.5 80.9 %collective-permute-done = bf16[64,3,128,128]{3,2,1,0:T(8,128)(2,1)} collective-permute-done((bf16[64,3,128,128]{3,2,1,0:T(8,128)(2,1)}, bf16[64,3,128,128]{3,2,1,0:T(8,128)(2,1)}, u32[]{:S(2)}, u32[]{:S(2)}) %collective-permute-start) | collective-permute-done | bytes 6291488 | tf_op jit(solution)/shard_map/ppermute | solution.py:14
  185.4 8.0 %slice_convert_fusion.2 = (f32[64,1,128,128]{3,2,1,0:T(8,128)}, f32[64,1,128,128]{3,2,1,0:T(8,128)}, f32[64,1,128,128]{3,2,1,0:T(8,128)}) fusion(bf16[64,3,128,128]{3,2,1,0:T(8,128)(2,1)} %collective-permute-done), kind=kLoop, calls=%fused_computation.66 | loop fusion | flops 3145728 | bytes 18874368 | tf_op jit(solution)/shard_map/convert_element_type | solution.py:70
  193.4 5.7 %copy.1867 = f32[64,1,128,128]{2,3,0,1:T(8,128)} copy(f32[64,1,128,128]{3,2,1,0:T(8,128)} %get-tuple-element.84) | data formatting | bytes 8388608 | tf_op jit(solution)/shard_map/convert_element_type | solution.py:70
  199.1 5.6 %copy.1869 = f32[64,1,128,128]{2,3,0,1:T(8,128)} copy(f32[64,1,128,128]{3,2,1,0:T(8,128)} %get-tuple-element.85) | data formatting | bytes 8388608 | tf_op jit(solution)/shard_map/convert_element_type | solution.py:70
  204.7 5.6 %copy.1868 = f32[64,1,128,128]{2,3,0,1:T(8,128)} copy(f32[64,1,128,128]{3,2,1,0:T(8,128)} %get-tuple-element.86) | data formatting | bytes 8388608 | tf_op jit(solution)/shard_map/convert_element_type | solution.py:70
  210.3 14.5 %fusion.23 = (f32[64,128,128]{1,2,0:T(8,128)}, f32[64,128,128]{1,2,0:T(8,128)}, f32[64,128,128]{1,2,0:T(8,128)}) fusion(f32[64,1,128,128]{2,3,0,1:T(8,128)} %copy.1867, f32[64,1,128,128]{2,3,0,1:T(8,128)} %copy.1865, f32[64,1,128,128]{2,3,0,1:T(8,128)} %copy.1863, f32[64,1,128,128]{2,3,0,1:T(8,128)} %copy.1861, f32[128,128]{0,1:T(8,128)S(1)} %copy.1864, ...), kind=kLoop, calls=%fused_computation.40 | loop fusion | flops 22020096 | bytes 38010880 | tf_op jit(solution)/shard_map/add | solution.py:65
  224.8 17.5 %fusion.13 = f32[2,192,128,128]{2,3,0,1:T(8,128)} fusion(f32[64,128,128]{1,2,0:T(8,128)} %get-tuple-element.15, f32[64,128,128]{1,2,0:T(8,128)} %get-tuple-element.14, f32[64,128,128]{1,2,0:T(8,128)} %get-tuple-element.13, f32[1,128,128]{2,1,0:T(8,128)S(1)} %get-tuple-element.93, f32[1,128,128]{2,1,0:T(8,128)S(1)} %get-tuple-element.94), kind=kOutput, calls=%fused_computation.20 | convolution fusion | flops 4838162432 | bytes 37879808 | tf_op jit(solution)/shard_map/xca,mab->xmcb/dot_general | solution.py:31
  242.3 19.7 %multiply_add_fusion = (f32[1,192,128,128]{2,3,0,1:T(8,128)}, f32[1,192,128,128]{2,3,0,1:T(8,128)}) fusion(f32[2,192,128,128]{2,3,0,1:T(8,128)} %fusion.13, f32[128,128]{0,1:T(8,128)S(1)} %get-tuple-element.95, f32[128,128]{0,1:T(8,128)S(1)} %get-tuple-element.96), kind=kLoop, calls=%fused_computation.19 | loop fusion | flops 18874368 | bytes 50462720 | tf_op jit(solution)/shard_map/add | solution.py:36
  262.0 16.8 %fusion.17 = f32[2,64,192,128]{3,1,2,0:T(8,128)} fusion(f32[1,192,128,128]{2,3,0,1:T(8,128)} %get-tuple-element.6, f32[1,192,128,128]{2,3,0,1:T(8,128)} %get-tuple-element.5, f32[1,64,2,128]{3,1,2,0:T(8,128)S(1)} %get-tuple-element.92, f32[1,64,2,128]{3,1,2,0:T(8,128)S(1)} %get-tuple-element.91), kind=kOutput, calls=%fused_computation.27 | convolution fusion | flops 4838162432 | bytes 37879808 | tf_op jit(solution)/shard_map/yqxb,xmcb->yqmc/dot_general | solution.py:42
  278.8 6.8 %fusion.5 = bf16[2,64,256,128]{3,1,2,0:T(8,128)(2,1)S(1)} fusion(f32[2,64,192,128]{3,1,2,0:T(8,128)} %fusion.17, f32[2,64,64,128]{3,1,2,0:T(8,128)S(1)} %copy-done, f32[256]{0:T(256)S(1)} %mul.388), kind=kLoop, calls=%fused_computation.7 | loop fusion | flops 12582912 | bytes 25166848 | tf_op jit(solution)/shard_map/convert_element_type | solution.py:75
  287.4 5.3 fusion.81
  292.7 5.6 %fusion.79 = (bf16[2,1,256,128]{3,1,2,0:T(2,128)(2,1)S(1)}, bf16[2,1,256,128]{3,1,2,0:T(2,128)(2,1)S(1)}, bf16[2,1,256,128]{3,1,2,0:T(2,128)(2,1)S(1)}, bf16[2,1...) fusion(bf16[2,64,256,128]{3,1,2,0:T(8,128)(2,1)S(1)} %fusion.5), kind=kLoop, calls=%fused_computation.193 | loop fusion | bytes 4980736 | tf_op jit(solution)/shard_map/split | solution.py:78
  298.3 5.3 fusion.80
  306.0 109.9 %all_to_all.5 = bf16[64,2,1,256,128]{4,3,1,2,0:T(8,128)(2,1)S(1)} all-to-all(bf16[64,2,1,256,128]{4,3,1,2,0:T(8,128)(2,1)S(1)} %constant_dynamic-update-slice_fusion), channel_id=1, replica_groups=mesh['inp'=8,'tm'=8,'bl'=2] {'inp','tm'}, dimensions={0} | all-to-all | bytes 16777216 | tf_op jit(solution)/shard_map/all_to_all | solution.py:77
  415.9 7.3 %copy.1871 = bf16[8,64,2,8,4,128]{5,4,3,2,1,0:T(4,128)(2,1)} copy(bf16[8,64,2,8,4,128]{5,1,4,2,3,0:T(8,128)(2,1)S(1)} %bitcast.287) | data formatting | bytes 16777216 | tf_op jit(solution)/shard_map/transpose | solution.py:86
  423.2 14.4 %reshape.241 = bf16[8,64,8192]{2,1,0:T(8,128)(2,1)} reshape(bf16[8,64,2,8,4,128]{5,4,3,2,1,0:T(4,128)(2,1)} %copy.1871) | data formatting | bytes 16777216 | tf_op jit(solution)/shard_map/reshape | solution.py:86
  437.9 15.2 %stack_reshape.3 = bf16[1,8,64,8192]{3,2,1,0:T(8,128)(2,1)} reshape(bf16[8,64,2,8,4,128]{5,4,3,2,1,0:T(4,128)(2,1)} %copy.1871) | data formatting | bytes 16777216 | tf_op jit(solution)/shard_map/stack;reshape | solution.py:92
  453.0 8.4 %fusion.78 = (bf16[8,64,4096]{2,1,0:T(8,128)(2,1)}, bf16[8,64,4096]{2,1,0:T(8,128)(2,1)}) fusion(bf16[8,64,8192]{2,1,0:T(8,128)(2,1)} %reshape.241), kind=kLoop, calls=%fused_computation.192 | loop fusion | flops 2097152 | bytes 16777216 | tf_op jit(solution)/shard_map/slice | solution.py:88
  461.4 7.9 %maximum_bitcast_fusion.8 = bf16[1,8,64,8192]{3,2,1,0:T(8,128)(2,1)} fusion(bf16[8,64,4096]{2,1,0:T(8,128)(2,1)} %get-tuple-element.19, bf16[8,64,4096]{2,1,0:T(8,128)(2,1)} %get-tuple-element.18), kind=kLoop, calls=%fused_computation.25 | loop fusion | flops 16777216 | bytes 16777216 | tf_op jit(solution)/shard_map/stack | solution.py:92
  469.3 13.8 %pad_maximum_fusion = bf16[2,8,64,8192]{3,2,1,0:T(8,128)(2,1)} fusion(bf16[1,8,64,8192]{3,2,1,0:T(8,128)(2,1)} %maximum_bitcast_fusion.8, bf16[1,8,64,8192]{3,2,1,0:T(8,128)(2,1)} %stack_reshape.3), kind=kLoop, calls=%fused_computation.8 | loop fusion | flops 8388608 | bytes 33554432 | tf_op jit(solution)/shard_map/stack | solution.py:92
  483.1 42.5 %broadcast_multiply_fusion = f32[2,2,8,64,1024]{4,3,2,1,0:T(8,128)} fusion(bf16[1024,8192,1,1,1]{1,0,4,3,2:T(8,128)(2,1)} %bitcast.293, bf16[2,8192]{1,0:T(2,128)(2,1)S(1)} %compare_convert_fusion, bf16[2,8,64,8192]{3,2,1,0:T(8,128)(2,1)} %pad_maximum_fusion), kind=kOutput, calls=%fused_computation.59 | convolution fusion | flops 34378612736 | bytes 41975808 | tf_op jit(solution)/shard_map/xgpik,qk->xgpiq/dot_general | solution.py:95
  (92 shorter events, 11.8 us)
Async XLA Ops:
  6.5 476.5 %all-gather.2.cloned.1.call-start = ((), (), s32[]{:S(2)}) async-start(), calls=%async_computation.1 | async-start | bytes 25165824 | tf_op jit(solution)/shard_map/all_gather | solution.py:93
  37.3 13.4 %copy-start.2 = (s32[64]{0:T(128)S(1)}, s32[64]{0:T(128)}, u32[]{:S(2)}) copy-start(s32[64]{0:T(128)} %param.5) | copy-start | bytes 772
  37.3 13.5 %copy-start.1 = (f32[4,16384]{1,0:T(4,128)S(1)}, f32[4,16384]{1,0:T(4,128)}, u32[]{:S(2)}) copy-start(f32[4,16384]{1,0:T(4,128)} %param.4) | copy-start | bytes 786436
  45.5 140.0 %collective-permute-start = (bf16[64,3,128,128]{3,2,1,0:T(8,128)(2,1)}, bf16[64,3,128,128]{3,2,1,0:T(8,128)(2,1)}, u32[]{:S(2)}, u32[]{:S(2)}) collective-permute-start(bf16[64,3,128,128]{3,2,1,0:T(8,128)(2,1)} %slice.95), channel_id=1, source_target_pairs={{2,0},{4,2},{6,4},{8,6},{10,8},{12,10},{14,12},{3,1},{5,3},{7,5},{... | collective-permute-start | bytes 18874376 | tf_op jit(solution)/shard_map/ppermute | solution.py:14
  262.0 16.8 %copy-start = (f32[2,64,64,128]{3,1,2,0:T(8,128)S(1)}, f32[2,64,64,128]{3,1,2,0:T(8,128)}, u32[]{:S(2)}) copy-start(f32[2,64,64,128]{3,1,2,0:T(8,128)} %fusion.40) | copy-start | bytes 12582916
Sparse Core Ops, SparseCore 0:
  437.7 30.0 all-gather.1
